TPU v7x, 32 devices: a whole 2x2x4 slice. The times are simulated.
32 devices in a mesh: dp: 16 (over z, y, x), tensor: 2 (over core).
Axes of the slice: x: 2, y: 2, z: 4, core: 2. Of those that a mesh axis runs over, the one named last changes fastest.
Arguments:
- tokens: bfloat16 [1024, 16, 2560], P('tensor', 'dp'), may hold values from -6 to 6
- pre_gain: float32 [2560], replicated, may hold values from 0.25 to 1.75
- z_weight: bfloat16 [2560, 5120], P(None, 'tensor'), may hold values from -0.125 to 0.125
- x_weight: bfloat16 [2560, 5120], P(None, 'tensor'), may hold values from -0.125 to 0.125
- bc_weight: bfloat16 [2560, 256], replicated, may hold values from -0.125 to 0.125
- dt_weight: bfloat16 [2560, 80], P(None, 'tensor'), may hold values from -0.125 to 0.125
- conv_x_weight: float32 [4, 5120], P(None, 'tensor'), may hold values from -3 to 3
- conv_x_bias: float32 [5120], P('tensor'), may hold values from -3 to 3
- conv_bc_weight: float32 [4, 256], replicated, may hold values from -3 to 3
- conv_bc_bias: float32 [256], replicated, may hold values from -3 to 3
- dt_bias: float32 [80], P('tensor'), may hold values from -4 to -2
- decay_log: float32 [80], P('tensor'), may hold values from -6 to 0
- skip_gain: float32 [80], P('tensor'), may hold values from 0.5 to 2
- norm_gain: float32 [5120], P('tensor'), may hold values from 0.25 to 1.75
- out_weight: bfloat16 [5120, 2560], P('tensor'), may hold values from -0.078125 to 0.078125
- cotangent: bfloat16 [1024, 16, 2560], P('tensor', 'dp'), may hold values from -6 to 6
Outputs:
- layer_out: bfloat16 [1024, 16, 2560], P('tensor', 'dp')
- grad_tokens: bfloat16 [1024, 16, 2560], P('tensor', 'dp')
- grad_pre_gain: float32 [2560], replicated
- grad_z_weight: float32 [2560, 5120], P('dp', 'tensor')
- grad_x_weight: float32 [2560, 5120], P('dp', 'tensor')
- grad_bc_weight: float32 [2560, 256], P('dp')
- grad_dt_weight: float32 [2560, 80], P('dp', 'tensor')
- grad_conv_x_weight: float32 [4, 5120], P(None, 'tensor')
- grad_conv_x_bias: float32 [5120], P('tensor')
- grad_conv_bc_weight: float32 [4, 256], replicated
- grad_conv_bc_bias: float32 [256], replicated
- grad_dt_bias: float32 [80], P('tensor')
- grad_decay_log: float32 [80], P('tensor')
- grad_skip_gain: float32 [80], P('tensor')
- grad_norm_gain: float32 [5120], P('tensor')
- grad_out_weight: float32 [5120, 2560], P('tensor', 'dp')
All inputs are finite; a program needn't handle non-finite values.
Results may differ from a plain program's by a relative error of at most 0.012.
The roundings to bfloat16 on the way count: a program that leaves them out, or rounds other values in their place, can miss the bound.
Values may be sent and summed in bfloat16 or wider, within the bound.
A program may use at most 384 MiB of HBM per device.

v0:
```python
import jax
import jax.numpy as jnp
import numpy as np
from jax import lax
from jax.sharding import PartitionSpec as P

N = 128
Q = 256
EPSILON = 1e-05
PRECISE = lax.Precision.HIGHEST
BOTH = ("dp", "tensor")
F32 = jnp.float32
BF16 = jnp.bfloat16


def causal_conv(series, kernel, offsets):
    taps = kernel.shape[0]
    length = series.shape[0]
    padding = [(taps - 1, 0)] + [(0, 0)] * (series.ndim - 1)
    padded = jnp.pad(series, padding)
    summed = offsets + kernel[0] * padded[0:length]
    for tap_index in range(1, taps):
        summed = summed + kernel[tap_index] * padded[tap_index : tap_index + length]
    return jax.nn.silu(summed)


def state_space(inputs, steps, rates, b_proj, c_proj):
    length, heads, width = inputs.shape
    blocks = length // Q
    x_blocks = inputs.reshape(blocks, Q, heads, width)
    dt_blocks = steps.reshape(blocks, Q, heads)
    b_blocks = b_proj.reshape(blocks, Q, -1)
    c_blocks = c_proj.reshape(blocks, Q, -1)
    cumulative = jnp.cumsum(dt_blocks * rates, axis=1)
    by_head = jnp.transpose(cumulative, (0, 2, 1))
    spread = by_head[:, :, :, None] - by_head[:, :, None, :]
    causal = jnp.arange(Q)[:, None] >= jnp.arange(Q)[None, :]
    decay = jnp.exp(jnp.where(causal, spread, -jnp.inf))
    scores = jnp.einsum("kin,kjn->kij", c_blocks, b_blocks, precision=PRECISE)
    mixing = decay * scores[:, None] * jnp.transpose(dt_blocks, (0, 2, 1))[:, :, None, :]
    within = jnp.einsum("khij,kjhp->kihp", mixing, x_blocks, precision=PRECISE)
    to_end = jnp.exp(cumulative[:, -1:, :] - cumulative) * dt_blocks
    weighted = x_blocks * to_end[..., None]
    states = jnp.einsum("kjhp,kjn->khpn", weighted, b_blocks, precision=PRECISE)
    block_decay = jnp.exp(cumulative[:, -1, :])

    def advance(carried, element):
        factor, fresh = element
        return (carried * factor[:, None, None] + fresh, carried)

    _, entering = lax.scan(advance, jnp.zeros_like(states[0]), (block_decay, states))
    across = (
        jnp.einsum("kin,khpn->kihp", c_blocks, entering, precision=PRECISE)
        * jnp.exp(cumulative)[..., None]
    )
    return (within + across).reshape(length, heads, width)


def scan_part(x_in, b_proj, c_proj, dt_raw, conv_weight, conv_bias, dt_bias, decay_log, skip_gain):
    length = x_in.shape[0]
    heads = dt_bias.shape[0]
    conv_out = causal_conv(x_in, conv_weight, conv_bias).reshape(length, heads, -1)
    steps = jax.nn.softplus(dt_raw + dt_bias)
    result = (
        state_space(conv_out, steps, -jnp.exp(decay_log), b_proj, c_proj)
        + skip_gain[:, None] * conv_out
    )
    return result.reshape(length, -1)


def mm(a, b, dims, out=F32):
    return lax.dot_general(a, b, (dims, ((), ())), preferred_element_type=out)


def bit_orders(count):
    bits = count.bit_length() - 1
    rest = list(range(bits - 1, 1, -1))
    return ([0, 1][:bits] + rest, [1, 0][-bits:] + rest if bits > 1 else [0])


def solution(mesh):
    count = mesh.shape["dp"]
    orders = bit_orders(count)
    levels = len(orders[0])
    tables = np.zeros((2, count), np.int32)
    for side in range(2):
        for place in range(count):
            tables[side, place] = sum(
                ((place >> levels - 1 - k & 1) << orders[side][k] for k in range(levels))
            )
    swaps = []
    for k in range(levels):
        swaps.append(
            [(d * 2 + t, (d ^ 1 << orders[t][k]) * 2 + t) for d in range(count) for t in range(2)]
        )
    flip = [(0, 1), (1, 0)]

    def other(value):
        return lax.ppermute(value, "tensor", flip)

    def pair_sum(value):
        return value + other(value)

    def level(k, values):
        half = values.shape[0] // 2
        came = lax.ppermute(values[half:].astype(BF16), BOTH, swaps[k])
        return values[:half] + came.astype(F32)

    def scatter_product(left, right):
        half = left.shape[0] // 2
        send = mm(left[half:], right, ((1,), (0,)), BF16)
        came = lax.ppermute(send, BOTH, swaps[0])
        keep = lax.optimization_barrier(mm(left[:half], right, ((1,), (0,))))
        total = keep + came.astype(F32)
        for k in range(1, levels):
            total = level(k, total)
        return total

    def body(
        tokens,
        pre_gain,
        z_weight,
        x_weight,
        bc_weight,
        dt_weight,
        conv_x_weight,
        conv_x_bias,
        conv_bc_weight,
        conv_bc_bias,
        dt_bias,
        decay_log,
        skip_gain,
        norm_gain,
        out_weight,
        cotangent,
    ):
        rows, _, width = tokens.shape
        inner_total = z_weight.shape[1] * 2
        me = lax.axis_index("dp")
        side = lax.axis_index("tensor")
        own_tokens = tokens[:, 0]
        own_grad = cotangent[:, 0]
        far_tokens = other(own_tokens)
        far_grad = other(own_grad)

        def join(own, far):
            return jnp.where(
                side == 0, jnp.concatenate([own, far], 0), jnp.concatenate([far, own], 0)
            )

        def own_half(value):
            return lax.dynamic_slice_in_dim(value, side * rows, rows, 0)

        def far_half(value):
            return lax.dynamic_slice_in_dim(value, (1 - side) * rows, rows, 0)

        grad_all = join(own_grad, far_grad)
        token_all = join(own_tokens, far_tokens).astype(F32)
        scale_all = lax.rsqrt(jnp.mean(token_all * token_all, axis=-1, keepdims=True) + EPSILON)
        normed = (token_all * scale_all * pre_gain).astype(BF16)
        places = jnp.where(side == 0, jnp.asarray(tables[0]), jnp.asarray(tables[1])) ^ me

        def travel_order(value):
            turned = lax.optimization_barrier(value.T).reshape(count, width // count, -1)
            return turned[places].reshape(width, -1)

        normed_turned = travel_order(normed)
        grad_turned = travel_order(grad_all)
        gate_in = mm(normed, z_weight, ((1,), (0,)))
        x_in = mm(normed, x_weight, ((1,), (0,)))
        bc_in = mm(normed, bc_weight, ((1,), (0,)))
        dt_raw = mm(normed, dt_weight, ((1,), (0,)))
        bc_conv, conv_back = jax.vjp(causal_conv, bc_in, conv_bc_weight, conv_bc_bias)
        y, scan_back = jax.vjp(
            scan_part,
            x_in,
            bc_conv[:, :N],
            bc_conv[:, N:],
            dt_raw,
            conv_x_weight,
            conv_x_bias,
            dt_bias,
            decay_log,
            skip_gain,
        )
        sig = jax.nn.sigmoid(gate_in)
        mixed = y * gate_in * sig
        squares = pair_sum(jnp.sum(mixed * mixed, axis=-1, keepdims=True))
        gate_scale = lax.rsqrt(squares / inner_total + EPSILON)
        gated = (mixed * gate_scale * norm_gain).astype(BF16)
        grad_out = scatter_product(grad_turned, gated).T
        d_gated = mm(grad_all, out_weight, ((1,), (1,)))
        grad_norm = jnp.sum(d_gated * mixed * gate_scale, axis=0)
        scaled = d_gated * norm_gain
        inner_dot = pair_sum(jnp.sum(scaled * mixed, axis=-1, keepdims=True))
        d_mixed = gate_scale * scaled - mixed * gate_scale**3 * inner_dot / inner_total
        low_gate = (d_mixed * y * sig * (1.0 + gate_in * (1.0 - sig))).astype(BF16)
        grad_z = scatter_product(normed_turned, low_gate)
        far_branch = other(mm(far_half(gated), out_weight, ((1,), (0,)), BF16))
        own_branch = mm(own_half(gated), out_weight, ((1,), (0,)))
        token_f = own_tokens.astype(F32)
        layer_out = (token_f + own_branch + far_branch.astype(F32)).astype(BF16)
        (
            grad_x_in,
            grad_b,
            grad_c,
            grad_dt,
            grad_conv_w,
            grad_conv_b,
            grad_dt_bias,
            grad_decay,
            grad_skip,
        ) = scan_back(d_mixed * gate_in * sig)
        low_x = grad_x_in.astype(BF16)
        grad_xw = scatter_product(normed_turned, low_x)
        grad_bc_conv = pair_sum(jnp.concatenate([grad_b, grad_c], axis=-1))
        grad_bc_in, grad_conv_bc_w, grad_conv_bc_b = conv_back(grad_bc_conv)
        low_bc = grad_bc_in.astype(BF16)
        low_dt = grad_dt.astype(BF16)
        half_bc = lax.dynamic_slice_in_dim(low_bc, side * N, N, 1)
        grad_small = scatter_product(normed_turned, jnp.concatenate([half_bc, low_dt], axis=-1))
        own_bcw = grad_small[:, :N]
        far_bcw = other(own_bcw)
        grad_bcw = jnp.where(
            side == 0,
            jnp.concatenate([own_bcw, far_bcw], 1),
            jnp.concatenate([far_bcw, own_bcw], 1),
        )
        grad_dtw = grad_small[:, N:]

        def back(part):
            return (
                mm(part(low_gate), z_weight, ((1,), (1,)))
                + mm(part(low_x), x_weight, ((1,), (1,)))
                + mm(part(low_dt), dt_weight, ((1,), (1,)))
            )

        far_back = other(back(far_half))
        d_normed = back(own_half) + mm(own_half(low_bc), bc_weight, ((1,), (1,))) + far_back
        pre_scale = own_half(scale_all)
        grad_pre = lax.psum(jnp.sum(d_normed * token_f * pre_scale, axis=0), BOTH)
        gained = d_normed * pre_gain
        grad_tokens = (
            own_grad.astype(F32)
            + pre_scale * gained
            - token_f * pre_scale**3 * jnp.mean(gained * token_f, axis=-1, keepdims=True)
        )
        (
            grad_norm,
            grad_conv_w,
            grad_conv_b,
            grad_conv_bc_w,
            grad_conv_bc_b,
            grad_dt_bias,
            grad_decay,
            grad_skip,
        ) = lax.psum(
            (
                grad_norm,
                grad_conv_w,
                grad_conv_b,
                grad_conv_bc_w,
                grad_conv_bc_b,
                grad_dt_bias,
                grad_decay,
                grad_skip,
            ),
            "dp",
        )
        return (
            layer_out[:, None],
            grad_tokens.astype(BF16)[:, None],
            grad_pre,
            grad_z,
            grad_xw,
            grad_bcw,
            grad_dtw,
            grad_conv_w,
            grad_conv_b,
            grad_conv_bc_w,
            grad_conv_bc_b,
            grad_dt_bias,
            grad_decay,
            grad_skip,
            grad_norm,
            grad_out,
        )

    in_specs = (
        P("tensor", "dp", None),
        P(),
        P(None, "tensor"),
        P(None, "tensor"),
        P(),
        P(None, "tensor"),
        P(None, "tensor"),
        P("tensor"),
        P(),
        P(),
        P("tensor"),
        P("tensor"),
        P("tensor"),
        P("tensor"),
        P("tensor", None),
        P("tensor", "dp", None),
    )
    out_specs = (
        P("tensor", "dp", None),
        P("tensor", "dp", None),
        P(),
        P("dp", "tensor"),
        P("dp", "tensor"),
        P("dp", None),
        P("dp", "tensor"),
        P(None, "tensor"),
        P("tensor"),
        P(),
        P(),
        P("tensor"),
        P("tensor"),
        P("tensor"),
        P("tensor"),
        P("tensor", "dp"),
    )
    return jax.shard_map(body, mesh=mesh, in_specs=in_specs, out_specs=out_specs, check_vma=False)
```

profile of v0, /device:TPU:0, one launch (start us, length us, event | category | flops | bytes accessed | tf_op | source)
XLA Modules:
  0.0 1383.1 jit_solution(2713497785616016151)
XLA Ops:
  33.4 18.3 %fusion.127 = f32[1024,2560]{1,0:T(8,128)S(1)} fusion(bf16[1024,2560]{1,0:T(8,128)(2,1)} %copy-done.6, bf16[2560,2560]{1,0:T(8,128)(2,1)} %param.25), kind=kOutput, calls=%fused_computation.256 | convolution fusion | flops 13421772800 | bytes 28835840 | tf_op jit(solution)/shard_map/dot_general | solution.py:72
  62.3 15.7 %reshape.298 = f32[4,256,40,64]{3,2,1,0:T(8,128)} reshape(f32[1024,2560]{1,0:T(8,128)} %get-tuple-element.386) | data formatting | bytes 20971520 | tf_op jit(solution)/shard_map/jvp()/reshape;jvp()/reshape | solution.py:30
  78.0 16.1 %copy.169 = f32[4,256,40,64]{1,3,2,0:T(8,128)} copy(f32[4,256,40,64]{3,2,1,0:T(8,128)} %reshape.298) | data formatting | bytes 20971520 | tf_op jit(solution)/shard_map/jvp()/reshape;jvp()/reshape | solution.py:30
  142.5 50.2 %bitcast_add_fusion.3 = f32[4,256,40,64]{1,3,2,0:T(8,128)} fusion(f32[4,256,40,64]{1,3,2,0:T(8,128)S(1)} %fusion.130, f32[4,256,40]{1,2,0:T(8,128)S(1)} %get-tuple-element.412, f32[4,256,40,64]{1,3,2,0:T(8,128)} %copy.169, f32[4,40,256]{2,1,0:T(8,128)S(1)} %copy.168, f32[4,256,256]{2,1,0:T(8,128)S(1)} %fusion.129, f32[4,40,256]{2,1,0:T(8,128)S(1)} %copy-done.52, ...), kind=kOutput, calls=%fused_computation.51 | convolution fusion | flops 8100249600 | bytes 33062912 | tf_op jit(solution)/shard_map/jvp(khij,kjhp->kihp)/dot_general | solution.py:41
  192.7 15.1 %copy.202 = f32[4,256,40,64]{3,2,1,0:T(8,128)} copy(f32[4,256,40,64]{1,3,2,0:T(8,128)} %bitcast_add_fusion.3) | data formatting | bytes 20971520 | tf_op jit(solution)/shard_map/jvp()/reshape | solution.py:56
  207.8 17.7 %reshape.296 = f32[1024,2560]{1,0:T(8,128)} reshape(f32[4,256,40,64]{3,2,1,0:T(8,128)} %copy.202) | data formatting | bytes 20971520 | tf_op jit(solution)/shard_map/jvp()/reshape | solution.py:56
  225.5 27.6 %multiply_reduce_fusion.11 = (f32[1024]{0:T(1024)S(1)}, f32[1024,2560]{1,0:T(8,128)}, f32[1024,2560]{1,0:T(8,128)}) fusion(f32[1024,2560]{1,0:T(8,128)} %reshape.296, f32[1024,2560]{1,0:T(8,128)} %get-tuple-element.387, f32[2560]{0:T(1024)S(1)} %mul.590, bf16[1024,2560]{1,0:T(8,128)(2,1)} %copy-done.6, bf16[2560,2560]{1,0:T(8,128)(2,1)} %param.24), kind=kOutput, calls=%fused_computation.65 | convolution fusion | flops 13455850496 | bytes 60307456 | tf_op jit(solution)/shard_map/dot_general | solution.py:72
  299.6 24.9 %multiply_reduce_fusion.2 = (f32[2560]{0:T(1024)}, f32[1024]{0:T(1024)S(1)}, f32[1024,2560]{1,0:T(8,128)}) fusion(f32[1024,2560]{1,0:T(8,128)} %get-tuple-element.385, f32[1024]{0:T(1024)S(1)} %bitcast.325, f32[2560]{0:T(1024)S(1)} %copy-done.79, bf16[2560,2560]{1,0:T(8,128)(2,1)} %param.36, bf16[512,2560]{1,0:T(8,128)(2,1)} %collective-permute-done.3, ...), kind=kOutput, calls=%fused_computation.52 | convolution fusion | flops 13461091328 | bytes 39350272 | tf_op jit(solution)/shard_map/dot_general | solution.py:72
  325.7 26.4 %multiply_reduce_fusion.3 = (f32[2560]{0:T(1024)}, f32[1024,2560]{1,0:T(8,128)}, bf16[1024,2560]{1,0:T(8,128)(2,1)}, bf16[1024,2560]{1,0:T(8,128)(2,1)}) fusion(f32[1024,2560]{1,0:T(8,128)} %get-tuple-element.387, f32[1024,2560]{1,0:T(8,128)} %get-tuple-element.420, f32[1024]{0:T(1024)S(1)} %bitcast.323, f32[1024,2560]{1,0:T(8,128)} %get-tuple-element.385, ...), kind=kLoop, calls=%fused_computation.53 | loop fusion | flops 76019200 | bytes 73443328 | tf_op jit(solution)/shard_map/transpose(jvp())/reduce_sum | solution.py:66
  376.6 16.2 %fusion.38 = f32[4,40,64,128]{3,2,1,0:T(8,128)} fusion(f32[4,256,128,1]{2,1,3,0:T(8,128)S(1)} %bitcast.284, f32[4,256,40,64]{1,0,3,2:T(4,128)} %reshape.256, f32[4,256,40]{1,2,0:T(8,128)S(1)} %copy-done.43), kind=kOutput, calls=%fused_computation.83 | convolution fusion | flops 4029153280 | bytes 16416768 | tf_op jit(solution)/shard_map/transpose(jvp(kin,khpn->kihp))/dot_general | solution.py:53
  392.8 19.6 %fusion.69 = f32[4,256,128]{2,1,0:T(8,128)} fusion(f32[4,40,64,128]{3,2,1,0:T(8,128)} %get-tuple-element.541, f32[4,256,40,64]{1,0,3,2:T(4,128)S(1)} %copy-done.2, f32[4,256,40]{1,2,0:T(8,128)S(1)} %copy-done.43), kind=kOutput, calls=%fused_computation.141 | convolution fusion | flops 4029153280 | bytes 16416768 | tf_op jit(solution)/shard_map/transpose(jvp(kin,khpn->kihp))/dot_general | solution.py:53
  415.3 15.7 %while.35 = (s32[]{:T(128)}, f32[40,64,128]{2,1,0:T(8,128)S(1)}, f32[4,40]{1,0:T(4,128)S(1)}, f32[4,40,64,128]{3,2,1,0:T(8,128)}, f32[4,40,64,128]{3,2,1,0:T(8,1...) while((s32[]{:T(128)}, f32[40,64,128]{2,1,0:T(8,128)S(1)}, ...), condition=%wide.region_9.10_spmd.clone, body=%wide.region_7.9_spmd.clone.sunk | while | flops 1966044 | bytes 7865420 | solution.py:51
  431.1 21.2 %fusion.70 = f32[4,256,128]{2,1,0:T(8,128)} fusion(f32[4,40,64,128]{3,2,1,0:T(8,128)} %get-tuple-element.193, f32[4,256,40,64]{1,3,2,0:T(8,128)} %copy.169, f32[4,256,40]{1,2,0:T(8,128)S(1)} %copy-done.38), kind=kOutput, calls=%fused_computation.142 | convolution fusion | flops 4029153280 | bytes 16416768 | tf_op jit(solution)/shard_map/transpose(jvp(kjhp,kjn->khpn))/dot_general | solution.py:44
  477.3 66.4 %fusion.10 = (f32[4,40,256]{2,1,0:T(8,128)}, f32[4,40,256]{2,1,0:T(8,128)}, f32[4,40,256]{2,1,0:T(8,128)}, f32[4,256,256]{2,1,0:T(8,128)}) fusion(f32[4,40,256]{2,1,0:T(8,128)} %copy-done.54, f32[4,256,256]{2,1,0:T(8,128)} %copy-done.44, f32[4,40,256]{2,1,0:T(8,128)} %get-tuple-element.410, pred[256,256]{1,0:T(8,128)(4,1)S(1)} %copy-done.71, ...), kind=kOutput, calls=%fused_computation.22 | convolution fusion | flops 8188993536 | bytes 23953408 | tf_op jit(solution)/shard_map/transpose(jvp(khij,kjhp->kihp))/dot_general | solution.py:41
  543.8 38.2 %bitcast_add_fusion.2 = f32[4,256,40,64]{1,3,2,0:T(8,128)} fusion(f32[4,256,40,64]{1,3,2,0:T(8,128)S(1)} %copy-done.17, f32[4,256,40]{1,2,0:T(8,128)S(1)} %copy-done.39, f32[4,40,256]{2,1,0:T(8,128)S(1)} %copy-done.55, f32[4,256,256]{2,1,0:T(8,128)S(1)} %copy-done.45, f32[4,40,256]{2,1,0:T(8,128)S(1)} %copy-done.53, pred[256,256]{1,0:T(8,128)(4,1)S(1)} %copy-done.71, ...), kind=kOutput, calls=%fused_computation.50 | convolution fusion | flops 8100249600 | bytes 33062912 | tf_op jit(solution)/shard_map/transpose(jvp(khij,kjhp->kihp))/dot_general | solution.py:41
  581.9 15.1 %copy.203 = f32[4,256,40,64]{3,2,1,0:T(8,128)} copy(f32[4,256,40,64]{1,3,2,0:T(8,128)} %bitcast_add_fusion.2) | data formatting | bytes 20971520 | tf_op jit(solution)/shard_map/transpose(jvp())/reshape | solution.py:30
  597.0 17.7 %reshape.297 = f32[1024,2560]{1,0:T(8,128)} reshape(f32[4,256,40,64]{3,2,1,0:T(8,128)} %copy.203) | data formatting | bytes 20971520 | tf_op jit(solution)/shard_map/transpose(jvp())/reshape | solution.py:30
  614.7 25.3 %multiply_reduce_fusion.7 = (f32[2560]{0:T(1024)S(1)}, f32[2560]{0:T(1024)S(1)}, f32[2560]{0:T(1024)S(1)}, f32[2560]{0:T(1024)S(1)}, f32[2560]{0:T(1024)}, /*index=5*/f32[1024,2560]{1,0:T(8,128)S(1)}) fusion(f32[1024,2560]{1,0:T(8,128)} %copy-done.7, f32[1024,2560]{1,0:T(8,128)} %get-tuple-element.387, f32[1024,2560]{1,0:T(8,128)} %reshape.297, ...), kind=kLoop, calls=%fused_computation.57 | loop fusion | flops 52416000 | bytes 52490240 | tf_op jit(solution)/shard_map/transpose(jvp())/reduce_sum | solution.py:23
  640.1 15.1 %broadcast_multiply_fusion = (f32[1024,2560]{1,0:T(8,128)}, f32[1024,2560]{1,0:T(8,128)}, f32[1024,2560]{1,0:T(8,128)}, f32[1024,2560]{1,0:T(8,128)}) fusion(f32[1024,2560]{1,0:T(8,128)S(1)} %get-tuple-element.381, f32[2560]{0:T(1024)S(1)} %copy-done.63, f32[2560]{0:T(1024)S(1)} %copy-done.59, f32[2560]{0:T(1024)S(1)} %copy-done.61, f32[2560]{0:T(1024)S(1)} %copy-done.65), kind=kLoop, calls=%fused_computation.110 | loop fusion | flops 10485760 | bytes 52469760 | tf_op jit(solution)/shard_map/transpose(jvp())/mul | solution.py:23
  655.2 15.2 %fusion.28 = bf16[1024,2560]{1,0:T(8,128)(2,1)S(1)} fusion(f32[1024,2560]{1,0:T(8,128)} %get-tuple-element.395, f32[1024,2560]{1,0:T(8,128)} %get-tuple-element.396, f32[1024,2560]{1,0:T(8,128)} %get-tuple-element.397, f32[1024,2560]{1,0:T(8,128)} %get-tuple-element.394), kind=kLoop, calls=%fused_computation.47 | loop fusion | flops 10485760 | bytes 47185920 | tf_op jit(solution)/shard_map/convert.13
  794.7 16.3 %add_add_fusion = f32[512,2560]{1,0:T(8,128)} fusion(f32[512,2560]{1,0:T(8,128)} %fusion.94, f32[512,2560]{1,0:T(8,128)} %fusion.59, bf16[2560,2560]{1,0:T(8,128)(2,1)} %param.24, bf16[1024,2560]{1,0:T(8,128)(2,1)} %get-tuple-element.392, s32[]{:T(128)S(6)} %select_n.74), kind=kOutput, calls=%fused_computation.104 | convolution fusion | flops 6713507840 | bytes 31457284 | tf_op jit(solution)/shard_map/dot_general | solution.py:72
  814.2 96.2 %collective-permute-done.15 = bf16[1280,168]{0,1:T(8,128)(2,1)S(1)} collective-permute-done((bf16[1280,168]{0,1:T(8,128)(2,1)S(1)}, bf16[1280,168]{0,1:T(8,128)(2,1)S(1)}, u32[]{:S(2)}, u32[]{:S(2)}) %collective-permute-start.15) | collective-permute-done | bytes 430112 | tf_op jit(solution)/shard_map/ppermute | solution.py:112
  948.0 18.1 %fusion.46 = (f32[2560]{0:T(1024)S(1)}, f32[512]{0:T(512)S(1)}, f32[512,2560]{1,0:T(8,128)}) fusion(f32[512]{0:T(512)S(1)} %copy-done.77, bf16[512,1,2560]{2,0,1:T(8,128)(2,1)} %param.22, f32[2560]{0:T(1024)S(1)} %copy-done.73, f32[512,2560]{1,0:T(8,128)} %collective-permute-done.6, f32[512,2560]{1,0:T(8,128)} %fusion.81, f32[512,2560]{1,0:T(8,128)} %fusion.96, ...), kind=kOutput, calls=%fused_computation.101 | convolution fusion | flops 6725301248 | bytes 44589060 | tf_op jit(solution)/shard_map/dot_general | solution.py:72
  966.1 74.9 %psum.63 = f32[2560]{0:T(1024)} all-reduce(f32[2560]{0:T(1024)S(1)} %get-tuple-element.331), channel_id=1, replica_groups=mesh['dp'=16,'tensor'=2] {'dp','tensor'}, use_global_device_ids=true, to_apply=%region_21.22 | all-reduce | flops 2560 | bytes 20480 | tf_op jit(solution)/shard_map/psum | solution.py:241
  1101.3 22.3 %collective-permute-done.12 = bf16[640,2560]{1,0:T(8,128)(2,1)} collective-permute-done((bf16[640,2560]{1,0:T(8,128)(2,1)}, bf16[640,2560]{1,0:T(8,128)(2,1)}, u32[]{:S(2)}, u32[]{:S(2)}) %collective-permute-start.12) | collective-permute-done | bytes 3276832 | tf_op jit(solution)/shard_map/ppermute | solution.py:106
  1134.0 24.6 %collective-permute-done.8 = bf16[640,2560]{1,0:T(8,128)(2,1)} collective-permute-done((bf16[640,2560]{1,0:T(8,128)(2,1)}, bf16[640,2560]{1,0:T(8,128)(2,1)}, u32[]{:S(2)}, u32[]{:S(2)}) %collective-permute-start.8) | collective-permute-done | bytes 3276832 | tf_op jit(solution)/shard_map/ppermute | solution.py:106
  1167.6 74.3 %collective-permute-done.22 = bf16[320,2560]{1,0:T(8,128)(2,1)S(1)} collective-permute-done((bf16[320,2560]{1,0:T(8,128)(2,1)S(1)}, bf16[320,2560]{1,0:T(8,128)(2,1)S(1)}, u32[]{:S(2)}, u32[]{:S(2)}) %collective-permute-start.22) | collective-permute-done | bytes 1638432 | tf_op jit(solution)/shard_map/ppermute | solution.py:106
  1244.6 32.5 %collective-permute-done.13 = bf16[320,2560]{1,0:T(8,128)(2,1)S(1)} collective-permute-done((bf16[320,2560]{1,0:T(8,128)(2,1)S(1)}, bf16[320,2560]{1,0:T(8,128)(2,1)S(1)}, u32[]{:S(2)}, u32[]{:S(2)}) %collective-permute-start.13) | collective-permute-done | bytes 1638432 | tf_op jit(solution)/shard_map/ppermute | solution.py:106
  1277.7 34.2 %collective-permute-done.9 = bf16[320,2560]{1,0:T(8,128)(2,1)S(1)} collective-permute-done((bf16[320,2560]{1,0:T(8,128)(2,1)S(1)}, bf16[320,2560]{1,0:T(8,128)(2,1)S(1)}, u32[]{:S(2)}, u32[]{:S(2)}) %collective-permute-start.9) | collective-permute-done | bytes 1638432 | tf_op jit(solution)/shard_map/ppermute | solution.py:106
  1312.5 17.0 %collective-permute-done.23 = bf16[160,2560]{1,0:T(8,128)(2,1)S(1)} collective-permute-done((bf16[160,2560]{1,0:T(8,128)(2,1)S(1)}, bf16[160,2560]{1,0:T(8,128)(2,1)S(1)}, u32[]{:S(2)}, u32[]{:S(2)}) %collective-permute-start.23) | collective-permute-done | bytes 819232 | tf_op jit(solution)/shard_map/ppermute | solution.py:106
  1330.8 16.2 %collective-permute-done.14 = bf16[160,2560]{1,0:T(8,128)(2,1)S(1)} collective-permute-done((bf16[160,2560]{1,0:T(8,128)(2,1)S(1)}, bf16[160,2560]{1,0:T(8,128)(2,1)S(1)}, u32[]{:S(2)}, u32[]{:S(2)}) %collective-permute-start.14) | collective-permute-done | bytes 819232 | tf_op jit(solution)/shard_map/ppermute | solution.py:106
  1348.3 16.1 %collective-permute-done.10 = bf16[160,2560]{1,0:T(8,128)(2,1)S(1)} collective-permute-done((bf16[160,2560]{1,0:T(8,128)(2,1)S(1)}, bf16[160,2560]{1,0:T(8,128)(2,1)S(1)}, u32[]{:S(2)}, u32[]{:S(2)}) %collective-permute-start.10) | collective-permute-done | bytes 819232 | tf_op jit(solution)/shard_map/ppermute | solution.py:106
  (453 shorter events, 475.4 us)
Async XLA Ops:
  7.2 86.9 %copy-start = (bf16[2560,256]{1,0:T(8,128)(2,1)S(1)}, bf16[2560,256]{1,0:T(8,128)(2,1)}, u32[]{:S(2)}) copy-start(bf16[2560,256]{1,0:T(8,128)(2,1)} %param.26) | copy-start | bytes 3932164
  7.2 1358.6 %all-reduce.23.cloned.1.call-start = ((), (), s32[]{:S(2)}) async-start(), calls=%async_computation | async-start | bytes 144384 | tf_op jit(solution)/shard_map/psum | solution.py:257
  7.2 6.1 collective-permute-start
  7.8 245.7 %collective-permute-start.3 = (bf16[512,2560]{1,0:T(8,128)(2,1)}, bf16[512,2560]{1,0:T(8,128)(2,1)}, u32[]{:S(2)}, u32[]{:S(2)}) collective-permute-start(bf16[512,2560]{1,0:T(8,128)(2,1)} %bitcast.296), channel_id=1, source_target_pairs={{0,1},{1,0},{2,3},{3,2},{4,5},{5,4},{6,7},{7,6},{8,9},{9,8},{10,11... | collective-permute-start | bytes 7864328 | tf_op jit(solution)/shard_map/ppermute | solution.py:99
  8.6 317.1 %copy-start.66 = (f32[2560]{0:T(1024)}, f32[2560]{0:T(1024)S(1)}, u32[]{:S(2)}) copy-start(f32[2560]{0:T(1024)S(1)} %mul.590) | copy-start | bytes 30724
  32.6 106.5 %copy-start.42 = (f32[4,256,40]{1,2,0:T(8,128)}, f32[4,256,40]{1,2,0:T(8,128)S(1)}, u32[]{:S(2)}) copy-start(f32[4,256,40]{1,2,0:T(8,128)S(1)} %get-tuple-element.412) | copy-start | bytes 491524
  253.0 46.6 %collective-permute-start.1 = (f32[1024,1]{0,1:T(1,128)S(1)}, f32[1024,1]{0,1:T(1,128)S(1)}, u32[]{:S(2)}, u32[]{:S(2)}) collective-permute-start(f32[1024,1]{0,1:T(1,128)S(1)} %bitcast.343), channel_id=1, source_target_pairs={{0,1},{1,0},{2,3},{3,2},{4,5},{5,4},{6,7},{7,6},{8,9},{9,8},{10,11... | collective-permute-start | bytes 12296 | tf_op jit(solution)/shard_map/ppermute | solution.py:99
  324.5 1.2 collective-permute-start.4
  761.0 280.0 %collective-permute-start.20 = (bf16[1280,2560]{1,0:T(8,128)(2,1)}, bf16[1280,2560]{1,0:T(8,128)(2,1)}, u32[]{:S(2)}, u32[]{:S(2)}) collective-permute-start(bf16[1280,2560]{1,0:T(8,128)(2,1)} %fusion.136), channel_id=1, source_target_pairs={{0,2},{1,5},{2,0},{3,7},{4,6},{5,1},{6,4},{7,3},{8,10},{9,13},{10,... | collective-permute-start | bytes 19660808 | tf_op jit(solution)/shard_map/ppermute | solution.py:112
  776.9 12.9 collective-permute-start.5
  777.2 274.5 %collective-permute-start.11 = (bf16[1280,2560]{1,0:T(8,128)(2,1)}, bf16[1280,2560]{1,0:T(8,128)(2,1)}, u32[]{:S(2)}, u32[]{:S(2)}) collective-permute-start(bf16[1280,2560]{1,0:T(8,128)(2,1)} %fusion.134), channel_id=1, source_target_pairs={{0,2},{1,5},{2,0},{3,7},{4,6},{5,1},{6,4},{7,3},{8,10},{9,13},{10,... | collective-permute-start | bytes 19660808 | tf_op jit(solution)/shard_map/ppermute | solution.py:112
  794.1 116.4 %collective-permute-start.15 = (bf16[1280,168]{0,1:T(8,128)(2,1)S(1)}, bf16[1280,168]{0,1:T(8,128)(2,1)S(1)}, u32[]{:S(2)}, u32[]{:S(2)}) collective-permute-start(bf16[1280,168]{0,1:T(8,128)(2,1)S(1)} %fusion.79), channel_id=1, source_target_pairs={{0,2},{1,5},{2,0},{3,7},{4,6},{5,1},{6,4},{7,3},{8,10},{9,13},{10,... | collective-permute-start | bytes 1290248 | tf_op jit(solution)/shard_map/ppermute | solution.py:112
  811.0 101.8 %copy-start.95 = (f32[40]{0:T(128)S(1)}, f32[40]{0:T(128)}, u32[]{:S(2)}) copy-start(f32[40]{0:T(128)} %param.33) | copy-start | bytes 484
  811.0 109.6 %copy-start.72 = (f32[2560]{0:T(1024)S(1)}, f32[2560]{0:T(1024)}, u32[]{:S(2)}) copy-start(f32[2560]{0:T(1024)} %get-tuple-element.376) | copy-start | bytes 30724
  811.0 137.0 %collective-permute-start.6 = (f32[512,2560]{1,0:T(8,128)}, f32[512,2560]{1,0:T(8,128)}, u32[]{:S(2)}, u32[]{:S(2)}) collective-permute-start(f32[512,2560]{1,0:T(8,128)} %add_add_fusion), channel_id=1, source_target_pairs={{0,1},{1,0},{2,3},{3,2},{4,5},{5,4},{6,7},{7,6},{8,9},{9,8},{10,11... | collective-permute-start | bytes 15728648 | tf_op jit(solution)/shard_map/ppermute | solution.py:99
  811.0 122.4 %collective-permute-start.2 = (bf16[512,2560]{1,0:T(8,128)(2,1)}, bf16[512,2560]{1,0:T(8,128)(2,1)}, u32[]{:S(2)}, u32[]{:S(2)}) collective-permute-start(bf16[512,2560]{1,0:T(8,128)(2,1)} %fusion.65), channel_id=1, source_target_pairs={{0,1},{1,0},{2,3},{3,2},{4,5},{5,4},{6,7},{7,6},{8,9},{9,8},{10,11... | collective-permute-start | bytes 7864328 | tf_op jit(solution)/shard_map/ppermute | solution.py:99
  910.6 6.0 collective-permute-start.16
  916.7 8.2 collective-permute-start.17
  925.1 4.6 collective-permute-start.18
  929.7 1.4 collective-permute-start.19
  931.1 138.4 %collective-permute-start.7 = (bf16[1280,2560]{1,0:T(8,128)(2,1)}, bf16[1280,2560]{1,0:T(8,128)(2,1)}, u32[]{:S(2)}, u32[]{:S(2)}) collective-permute-start(bf16[1280,2560]{1,0:T(8,128)(2,1)} %fusion.132), channel_id=1, source_target_pairs={{0,2},{1,5},{2,0},{3,7},{4,6},{5,1},{6,4},{7,3},{8,10},{9,13},{10,... | collective-permute-start | bytes 19660808 | tf_op jit(solution)/shard_map/ppermute | solution.py:112
  1048.9 43.5 %collective-permute-start.21 = (bf16[640,2560]{1,0:T(8,128)(2,1)S(1)}, bf16[640,2560]{1,0:T(8,128)(2,1)}, u32[]{:S(2)}, u32[]{:S(2)}) collective-permute-start(bf16[640,2560]{1,0:T(8,128)(2,1)S(1)} %slice.339), channel_id=1, source_target_pairs={{0,4},{1,3},{2,6},{3,1},{4,0},{5,7},{6,2},{7,5},{8,12},{9,11},{10,... | collective-permute-start | bytes 9830408 | tf_op jit(solution)/shard_map/ppermute | solution.py:106
  1069.5 54.1 %collective-permute-start.12 = (bf16[640,2560]{1,0:T(8,128)(2,1)}, bf16[640,2560]{1,0:T(8,128)(2,1)}, u32[]{:S(2)}, u32[]{:S(2)}) collective-permute-start(bf16[640,2560]{1,0:T(8,128)(2,1)} %slice.340), channel_id=1, source_target_pairs={{0,4},{1,3},{2,6},{3,1},{4,0},{5,7},{6,2},{7,5},{8,12},{9,11},{10,... | collective-permute-start | bytes 9830408 | tf_op jit(solution)/shard_map/ppermute | solution.py:106
  1087.4 71.3 %collective-permute-start.8 = (bf16[640,2560]{1,0:T(8,128)(2,1)}, bf16[640,2560]{1,0:T(8,128)(2,1)}, u32[]{:S(2)}, u32[]{:S(2)}) collective-permute-start(bf16[640,2560]{1,0:T(8,128)(2,1)} %slice.341), channel_id=1, source_target_pairs={{0,4},{1,3},{2,6},{3,1},{4,0},{5,7},{6,2},{7,5},{8,12},{9,11},{10,... | collective-permute-start | bytes 9830408 | tf_op jit(solution)/shard_map/ppermute | solution.py:106
  1100.3 141.5 %collective-permute-start.22 = (bf16[320,2560]{1,0:T(8,128)(2,1)S(1)}, bf16[320,2560]{1,0:T(8,128)(2,1)S(1)}, u32[]{:S(2)}, u32[]{:S(2)}) collective-permute-start(bf16[320,2560]{1,0:T(8,128)(2,1)S(1)} %slice.342), channel_id=1, source_target_pairs={{0,16},{1,17},{2,18},{3,19},{4,20},{5,21},{6,22},{7,23},{8,24},{9,... | collective-permute-start | bytes 4915208 | tf_op jit(solution)/shard_map/ppermute | solution.py:106
  1133.1 144.0 %collective-permute-start.13 = (bf16[320,2560]{1,0:T(8,128)(2,1)S(1)}, bf16[320,2560]{1,0:T(8,128)(2,1)S(1)}, u32[]{:S(2)}, u32[]{:S(2)}) collective-permute-start(bf16[320,2560]{1,0:T(8,128)(2,1)S(1)} %slice.343), channel_id=1, source_target_pairs={{0,16},{1,17},{2,18},{3,19},{4,20},{5,21},{6,22},{7,23},{8,24},{9,... | collective-permute-start | bytes 4915208 | tf_op jit(solution)/shard_map/ppermute | solution.py:106
  1164.4 112.7 %slice-start.7 = ((s8[6553600]{0:T(1024)(128)(4,1)}), s8[4194304]{0:T(1024)(128)(4,1)S(1)}, s32[]{:S(2)}) async-start(s8[6553600]{0:T(1024)(128)(4,1)} %bitcast.278), calls=%async_computation.8 | async-start | bytes 8388608
  1166.6 110.5 %slice-start.8 = ((s8[6553600]{0:T(1024)(128)(4,1)}), s8[2359296]{0:T(1024)(128)(4,1)S(1)}, s32[]{:S(2)}) async-start(s8[6553600]{0:T(1024)(128)(4,1)} %bitcast.278), calls=%async_computation.9 | async-start | bytes 4718592
  1166.7 145.2 %collective-permute-start.9 = (bf16[320,2560]{1,0:T(8,128)(2,1)S(1)}, bf16[320,2560]{1,0:T(8,128)(2,1)S(1)}, u32[]{:S(2)}, u32[]{:S(2)}) collective-permute-start(bf16[320,2560]{1,0:T(8,128)(2,1)S(1)} %slice.344), channel_id=1, source_target_pairs={{0,16},{1,17},{2,18},{3,19},{4,20},{5,21},{6,22},{7,23},{8,24},{9,... | collective-permute-start | bytes 4915208 | tf_op jit(solution)/shard_map/ppermute | solution.py:106
  1244.5 84.9 %collective-permute-start.23 = (bf16[160,2560]{1,0:T(8,128)(2,1)S(1)}, bf16[160,2560]{1,0:T(8,128)(2,1)S(1)}, u32[]{:S(2)}, u32[]{:S(2)}) collective-permute-start(bf16[160,2560]{1,0:T(8,128)(2,1)S(1)} %slice.345), channel_id=1, source_target_pairs={{0,8},{1,9},{2,10},{3,11},{4,12},{5,13},{6,14},{7,15},{8,0},{9,1},... | collective-permute-start | bytes 2457608 | tf_op jit(solution)/shard_map/ppermute | solution.py:106
  1277.6 69.4 %collective-permute-start.14 = (bf16[160,2560]{1,0:T(8,128)(2,1)S(1)}, bf16[160,2560]{1,0:T(8,128)(2,1)S(1)}, u32[]{:S(2)}, u32[]{:S(2)}) collective-permute-start(bf16[160,2560]{1,0:T(8,128)(2,1)S(1)} %slice.346), channel_id=1, source_target_pairs={{0,8},{1,9},{2,10},{3,11},{4,12},{5,13},{6,14},{7,15},{8,0},{9,1},... | collective-permute-start | bytes 2457608 | tf_op jit(solution)/shard_map/ppermute | solution.py:106
  1312.4 52.1 %collective-permute-start.10 = (bf16[160,2560]{1,0:T(8,128)(2,1)S(1)}, bf16[160,2560]{1,0:T(8,128)(2,1)S(1)}, u32[]{:S(2)}, u32[]{:S(2)}) collective-permute-start(bf16[160,2560]{1,0:T(8,128)(2,1)S(1)} %slice.347), channel_id=1, source_target_pairs={{0,8},{1,9},{2,10},{3,11},{4,12},{5,13},{6,14},{7,15},{8,0},{9,1},... | collective-permute-start | bytes 2457608 | tf_op jit(solution)/shard_map/ppermute | solution.py:106
  (108 other events, 2694.4 us)
Sparse Core Ops, SparseCore 0:
  930.5 107.5 all-reduce.22
where the time goes:
time: 1400 us; the launch traced here: 1380 us
  matrix products  484 us (35%)
  waiting for transfers between devices  342 us (24%)
  other arithmetic  233 us (17%)
  local copies, waits for them, and re-layouts  212 us (15%)
  blocking collectives  74.9 us (5%)
  starting transfers between devices  22 us (2%)
  between operations  16 us (1%)
    ppermute x12, waiting for transfers between devices, level(): came = lax.ppermute(values[half:].astype(BF16), BOTH, swaps[k])  245 us
    dot_general x22, matrix products, mm(): return lax.dot_general(a, b, (dims, ((), ())), preferred_element_type=out)  232 us
    dot_general x3, matrix products, state_space(): within = jnp.einsum('khij,kjhp->kihp', mixing, x_blocks, precision=PRECISE)  155 us
    ppermute x4, waiting for transfers between devices, scatter_product(): came = lax.ppermute(send, BOTH, swaps[0])  96.2 us
    psum x1, blocking collectives, body(): grad_pre = lax.psum(jnp.sum(d_normed * token_f * pre_scale, axis=0), BOTH)  74.9 us
    reshape x4, local copies, waits for them, and re-layouts, state_space(): x_blocks = inputs.reshape(blocks, Q, heads, width)  64.6 us
    dot_general x3, matrix products, state_space(): jnp.einsum('kin,khpn->kihp', c_blocks, entering, precision=PRECISE)  46.8 us
    reshape x3, local copies, waits for them, and re-layouts, state_space(): return (within + across).reshape(length, heads, width)  45.8 us
  transfers between devices with their start and end apart: 25, of which 14 were waited for; matrix products, arithmetic and copies ran while one was open for 33% of the time, Pallas kernels for 0%

commit v1 on v0

--- a/solution.py
+++ b/solution.py
@@ -238,7 +238,9 @@
         far_back = other(back(far_half))
         d_normed = back(own_half) + mm(own_half(low_bc), bc_weight, ((1,), (1,))) + far_back
         pre_scale = own_half(scale_all)
-        grad_pre = lax.psum(jnp.sum(d_normed * token_f * pre_scale, axis=0), BOTH)
+        grad_pre = lax.psum(
+            lax.psum(jnp.sum(d_normed * token_f * pre_scale, axis=0), "tensor"), "dp"
+        )
         gained = d_normed * pre_gain
         grad_tokens = (
             own_grad.astype(F32)

time: 1400 us -> 1330 us (0.950)
  blocking collectives: 74.9 us -> 4.14 us
    psum x1, blocking collectives: 74.9 us -> 4.14 us  [body(): lax.psum(jnp.sum(d_normed * token_f * pre_scale, axis=0), 'tensor')]
  transfers between devices with their start and end apart: 25 -> 25, of which waited for: 14 -> 15; matrix products, arithmetic and copies ran while one was open for 33% -> 37% of each run, Pallas kernels for 0% -> 0%
where the time goes in v1:
time: 1330 us; the launch traced here: 1320 us
  matrix products  487 us (37%)
  waiting for transfers between devices  334 us (25%)
  other arithmetic  237 us (18%)
  local copies, waits for them, and re-layouts  215 us (16%)
  starting transfers between devices  27.1 us (2%)
  between operations  15.8 us (1%)
    ppermute x12, waiting for transfers between devices, level(): came = lax.ppermute(values[half:].astype(BF16), BOTH, swaps[k])  243 us
    dot_general x22, matrix products, mm(): return lax.dot_general(a, b, (dims, ((), ())), preferred_element_type=out)  233 us
    dot_general x3, matrix products, state_space(): within = jnp.einsum('khij,kjhp->kihp', mixing, x_blocks, precision=PRECISE)  156 us
    ppermute x4, waiting for transfers between devices, scatter_product(): came = lax.ppermute(send, BOTH, swaps[0])  90.7 us
    reshape x4, local copies, waits for them, and re-layouts, state_space(): x_blocks = inputs.reshape(blocks, Q, heads, width)  64.4 us
    dot_general x3, matrix products, state_space(): jnp.einsum('kin,khpn->kihp', c_blocks, entering, precision=PRECISE)  46.9 us
    dot_general x3, matrix products, state_space(): states = jnp.einsum('kjhp,kjn->khpn', weighted, b_blocks, precision=PRECISE)  46.7 us
    reshape x3, local copies, waits for them, and re-layouts, state_space(): return (within + across).reshape(length, heads, width)  45.9 us
  transfers between devices with their start and end apart: 25, of which 15 were waited for; matrix products, arithmetic and copies ran while one was open for 37% of the time, Pallas kernels for 0%

profile of v1, /device:TPU:0, one launch (start us, length us, event | category | flops | bytes accessed | tf_op | source)
XLA Modules:
  0.0 1319.5 jit_solution(10102453437506843293)
XLA Ops:
  33.2 18.3 %fusion.127 = f32[1024,2560]{1,0:T(8,128)S(1)} fusion(bf16[1024,2560]{1,0:T(8,128)(2,1)} %copy-done.5, bf16[2560,2560]{1,0:T(8,128)(2,1)} %param.25), kind=kOutput, calls=%fused_computation.256 | convolution fusion | flops 13421772800 | bytes 28835840 | tf_op jit(solution)/shard_map/dot_general | solution.py:72
  62.0 15.7 %reshape.298 = f32[4,256,40,64]{3,2,1,0:T(8,128)} reshape(f32[1024,2560]{1,0:T(8,128)} %get-tuple-element.387) | data formatting | bytes 20971520 | tf_op jit(solution)/shard_map/jvp()/reshape;jvp()/reshape | solution.py:30
  77.7 15.9 %copy.169 = f32[4,256,40,64]{1,3,2,0:T(8,128)} copy(f32[4,256,40,64]{3,2,1,0:T(8,128)} %reshape.298) | data formatting | bytes 20971520 | tf_op jit(solution)/shard_map/jvp()/reshape;jvp()/reshape | solution.py:30
  141.9 50.2 %bitcast_add_fusion.3 = f32[4,256,40,64]{1,3,2,0:T(8,128)} fusion(f32[4,256,40,64]{1,3,2,0:T(8,128)S(1)} %fusion.130, f32[4,256,40]{1,2,0:T(8,128)S(1)} %get-tuple-element.413, f32[4,256,40,64]{1,3,2,0:T(8,128)} %copy.169, f32[4,40,256]{2,1,0:T(8,128)S(1)} %copy.168, f32[4,256,256]{2,1,0:T(8,128)S(1)} %fusion.129, f32[4,40,256]{2,1,0:T(8,128)S(1)} %copy-done.46, ...), kind=kOutput, calls=%fused_computation.51 | convolution fusion | flops 8100249600 | bytes 33062912 | tf_op jit(solution)/shard_map/jvp(khij,kjhp->kihp)/dot_general | solution.py:41
  192.1 15.2 %copy.202 = f32[4,256,40,64]{3,2,1,0:T(8,128)} copy(f32[4,256,40,64]{1,3,2,0:T(8,128)} %bitcast_add_fusion.3) | data formatting | bytes 20971520 | tf_op jit(solution)/shard_map/jvp()/reshape | solution.py:56
  207.3 17.7 %reshape.296 = f32[1024,2560]{1,0:T(8,128)} reshape(f32[4,256,40,64]{3,2,1,0:T(8,128)} %copy.202) | data formatting | bytes 20971520 | tf_op jit(solution)/shard_map/jvp()/reshape | solution.py:56
  224.9 27.6 %multiply_reduce_fusion.11 = (f32[1024]{0:T(1024)S(1)}, f32[1024,2560]{1,0:T(8,128)}, f32[1024,2560]{1,0:T(8,128)}) fusion(f32[1024,2560]{1,0:T(8,128)} %reshape.296, f32[1024,2560]{1,0:T(8,128)} %get-tuple-element.388, f32[2560]{0:T(1024)S(1)} %mul.590, bf16[1024,2560]{1,0:T(8,128)(2,1)} %copy-done.5, bf16[2560,2560]{1,0:T(8,128)(2,1)} %param.24), kind=kOutput, calls=%fused_computation.65 | convolution fusion | flops 13455850496 | bytes 60307456 | tf_op jit(solution)/shard_map/dot_general | solution.py:72
  299.4 24.9 %multiply_reduce_fusion.2 = (f32[2560]{0:T(1024)}, f32[1024]{0:T(1024)S(1)}, f32[1024,2560]{1,0:T(8,128)}) fusion(f32[1024,2560]{1,0:T(8,128)} %get-tuple-element.386, f32[1024]{0:T(1024)S(1)} %bitcast.327, f32[2560]{0:T(1024)S(1)} %copy-done.77, bf16[2560,2560]{1,0:T(8,128)(2,1)} %param.36, bf16[512,2560]{1,0:T(8,128)(2,1)} %collective-permute-done.3, ...), kind=kOutput, calls=%fused_computation.52 | convolution fusion | flops 13461091328 | bytes 39350272 | tf_op jit(solution)/shard_map/dot_general | solution.py:72
  325.5 26.4 %multiply_reduce_fusion.3 = (f32[2560]{0:T(1024)}, f32[1024,2560]{1,0:T(8,128)}, bf16[1024,2560]{1,0:T(8,128)(2,1)}, bf16[1024,2560]{1,0:T(8,128)(2,1)}) fusion(f32[1024,2560]{1,0:T(8,128)} %get-tuple-element.388, f32[1024,2560]{1,0:T(8,128)} %get-tuple-element.421, f32[1024]{0:T(1024)S(1)} %bitcast.325, f32[1024,2560]{1,0:T(8,128)} %get-tuple-element.386, ...), kind=kLoop, calls=%fused_computation.53 | loop fusion | flops 76019200 | bytes 73443328 | tf_op jit(solution)/shard_map/transpose(jvp())/reduce_sum | solution.py:66
  376.4 15.9 %fusion.38 = f32[4,40,64,128]{3,2,1,0:T(8,128)} fusion(f32[4,256,128,1]{2,1,3,0:T(8,128)S(1)} %bitcast.286, f32[4,256,40,64]{1,0,3,2:T(4,128)} %reshape.256, f32[4,256,40]{1,2,0:T(8,128)S(1)} %copy-done.41), kind=kOutput, calls=%fused_computation.83 | convolution fusion | flops 4029153280 | bytes 16416768 | tf_op jit(solution)/shard_map/transpose(jvp(kin,khpn->kihp))/dot_general | solution.py:53
  392.3 19.9 %fusion.69 = f32[4,256,128]{2,1,0:T(8,128)} fusion(f32[4,40,64,128]{3,2,1,0:T(8,128)} %get-tuple-element.542, f32[4,256,40,64]{1,0,3,2:T(4,128)S(1)} %copy-done.2, f32[4,256,40]{1,2,0:T(8,128)S(1)} %copy-done.41), kind=kOutput, calls=%fused_computation.141 | convolution fusion | flops 4029153280 | bytes 16416768 | tf_op jit(solution)/shard_map/transpose(jvp(kin,khpn->kihp))/dot_general | solution.py:53
  425.6 16.0 %while.35 = (s32[]{:T(128)}, f32[40,64,128]{2,1,0:T(8,128)S(1)}, f32[4,40]{1,0:T(4,128)S(1)}, f32[4,40,64,128]{3,2,1,0:T(8,128)}, f32[4,40,64,128]{3,2,1,0:T(8,1...) while((s32[]{:T(128)}, f32[40,64,128]{2,1,0:T(8,128)S(1)}, ...), condition=%wide.region_9.10_spmd.clone, body=%wide.region_7.9_spmd.clone.sunk | while | flops 1966044 | bytes 7865420 | solution.py:51
  441.7 21.0 %fusion.70 = f32[4,256,128]{2,1,0:T(8,128)} fusion(f32[4,40,64,128]{3,2,1,0:T(8,128)} %get-tuple-element.193, f32[4,256,40,64]{1,3,2,0:T(8,128)} %copy.169, f32[4,256,40]{1,2,0:T(8,128)S(1)} %copy-done.37), kind=kOutput, calls=%fused_computation.142 | convolution fusion | flops 4029153280 | bytes 16416768 | tf_op jit(solution)/shard_map/transpose(jvp(kjhp,kjn->khpn))/dot_general | solution.py:44
  462.7 14.9 %multiply_reduce_fusion.9 = (f32[4,256,40]{1,2,0:T(8,128)S(1)}, f32[4,256,40,64]{1,3,2,0:T(8,128)}) fusion(f32[4,256,40,64]{1,3,2,0:T(8,128)} %copy.169, f32[4,256,128,1]{2,1,3,0:T(8,128)S(1)} %bitcast.290, f32[4,40,64,128]{3,2,1,0:T(8,128)} %get-tuple-element.193), kind=kOutput, calls=%fused_computation.59 | convolution fusion | flops 4031733760 | bytes 26902528 | tf_op jit(solution)/shard_map/transpose(jvp(kjhp,kjn->khpn))/dot_general | solution.py:44
  477.8 65.5 %fusion.10 = (f32[4,40,256]{2,1,0:T(8,128)}, f32[4,40,256]{2,1,0:T(8,128)}, f32[4,40,256]{2,1,0:T(8,128)}, f32[4,256,256]{2,1,0:T(8,128)}) fusion(f32[4,40,256]{2,1,0:T(8,128)S(1)} %copy-done.49, f32[4,256,256]{2,1,0:T(8,128)S(1)} %copy-done.43, f32[4,40,256]{2,1,0:T(8,128)S(1)} %copy-done.47, pred[256,256]{1,0:T(8,128)(4,1)S(1)} %copy-done.65, ...), kind=kOutput, calls=%fused_computation.22 | convolution fusion | flops 8188993536 | bytes 23953408 | tf_op jit(solution)/shard_map/transpose(jvp(khij,kjhp->kihp))/dot_general | solution.py:41
  560.8 40.5 %bitcast_add_fusion.2 = f32[4,256,40,64]{1,3,2,0:T(8,128)} fusion(f32[4,256,40,64]{1,3,2,0:T(8,128)} %get-tuple-element.424, f32[4,256,40]{1,2,0:T(8,128)S(1)} %copy-done.37, f32[4,40,256]{2,1,0:T(8,128)} %copy-done.48, f32[4,256,256]{2,1,0:T(8,128)S(1)} %copy-done.44, f32[4,40,256]{2,1,0:T(8,128)} %get-tuple-element.411, ...), kind=kOutput, calls=%fused_computation.50 | convolution fusion | flops 8100249600 | bytes 33062912 | tf_op jit(solution)/shard_map/transpose(jvp(khij,kjhp->kihp))/dot_general | solution.py:41
  601.3 15.2 %copy.203 = f32[4,256,40,64]{3,2,1,0:T(8,128)} copy(f32[4,256,40,64]{1,3,2,0:T(8,128)} %bitcast_add_fusion.2) | data formatting | bytes 20971520 | tf_op jit(solution)/shard_map/transpose(jvp())/reshape | solution.py:30
  616.5 17.7 %reshape.297 = f32[1024,2560]{1,0:T(8,128)} reshape(f32[4,256,40,64]{3,2,1,0:T(8,128)} %copy.203) | data formatting | bytes 20971520 | tf_op jit(solution)/shard_map/transpose(jvp())/reshape | solution.py:30
  634.2 25.4 %multiply_reduce_fusion.7 = (f32[2560]{0:T(1024)}, f32[2560]{0:T(1024)}, f32[2560]{0:T(1024)}, f32[2560]{0:T(1024)}, f32[2560]{0:T(1024)}, /*index=5*/f32[1024,2560]{1,0:T(8,128)S(1)}) fusion(f32[1024,2560]{1,0:T(8,128)} %copy-done.6, f32[1024,2560]{1,0:T(8,128)} %get-tuple-element.388, f32[1024,2560]{1,0:T(8,128)} %reshape.297, ...), kind=kLoop, calls=%fused_computation.57 | loop fusion | flops 52416000 | bytes 52490240 | tf_op jit(solution)/shard_map/transpose(jvp())/reduce_sum | solution.py:23
  659.6 15.1 %broadcast_multiply_fusion = (f32[1024,2560]{1,0:T(8,128)}, f32[1024,2560]{1,0:T(8,128)}, f32[1024,2560]{1,0:T(8,128)}, f32[1024,2560]{1,0:T(8,128)}) fusion(f32[1024,2560]{1,0:T(8,128)S(1)} %get-tuple-element.382, f32[2560]{0:T(1024)S(1)} %copy-done.57, f32[2560]{0:T(1024)S(1)} %copy-done.53, f32[2560]{0:T(1024)S(1)} %copy-done.55, f32[2560]{0:T(1024)S(1)} %copy-done.59), kind=kLoop, calls=%fused_computation.110 | loop fusion | flops 10485760 | bytes 52469760 | tf_op jit(solution)/shard_map/transpose(jvp())/mul | solution.py:23
  677.8 15.1 %fusion.28 = bf16[1024,2560]{1,0:T(8,128)(2,1)S(1)} fusion(f32[1024,2560]{1,0:T(8,128)} %get-tuple-element.396, f32[1024,2560]{1,0:T(8,128)} %get-tuple-element.397, f32[1024,2560]{1,0:T(8,128)} %get-tuple-element.398, f32[1024,2560]{1,0:T(8,128)} %get-tuple-element.395), kind=kLoop, calls=%fused_computation.47 | loop fusion | flops 10485760 | bytes 47185920 | tf_op jit(solution)/shard_map/convert.13
  777.6 16.3 %add_add_fusion = f32[512,2560]{1,0:T(8,128)} fusion(f32[512,2560]{1,0:T(8,128)} %fusion.94, f32[512,2560]{1,0:T(8,128)} %fusion.59, bf16[2560,2560]{1,0:T(8,128)(2,1)} %param.24, bf16[1024,2560]{1,0:T(8,128)(2,1)} %get-tuple-element.393, s32[]{:T(128)S(6)} %select_n.74), kind=kOutput, calls=%fused_computation.104 | convolution fusion | flops 6713507840 | bytes 31457284 | tf_op jit(solution)/shard_map/dot_general | solution.py:72
  823.0 57.4 %collective-permute-done.15 = bf16[1280,168]{0,1:T(8,128)(2,1)S(1)} collective-permute-done((bf16[1280,168]{0,1:T(8,128)(2,1)S(1)}, bf16[1280,168]{0,1:T(8,128)(2,1)S(1)}, u32[]{:S(2)}, u32[]{:S(2)}) %collective-permute-start.15) | collective-permute-done | bytes 430112 | tf_op jit(solution)/shard_map/ppermute | solution.py:112
  917.9 18.1 %fusion.46 = (f32[2560]{0:T(1024)S(1)}, f32[512]{0:T(512)S(1)}, f32[512,2560]{1,0:T(8,128)}) fusion(f32[512]{0:T(512)S(1)} %copy-done.75, bf16[512,1,2560]{2,0,1:T(8,128)(2,1)} %param.22, f32[2560]{0:T(1024)S(1)} %copy-done.71, f32[512,2560]{1,0:T(8,128)} %collective-permute-done.6, f32[512,2560]{1,0:T(8,128)} %fusion.81, f32[512,2560]{1,0:T(8,128)} %fusion.96, ...), kind=kOutput, calls=%fused_computation.101 | convolution fusion | flops 6725301248 | bytes 44589060 | tf_op jit(solution)/shard_map/dot_general | solution.py:72
  968.1 33.3 %collective-permute-done.7 = bf16[1280,2560]{1,0:T(8,128)(2,1)} collective-permute-done((bf16[1280,2560]{1,0:T(8,128)(2,1)}, bf16[1280,2560]{1,0:T(8,128)(2,1)}, u32[]{:S(2)}, u32[]{:S(2)}) %collective-permute-start.7) | collective-permute-done | bytes 6553632 | tf_op jit(solution)/shard_map/ppermute | solution.py:112
  1059.7 22.6 %collective-permute-done.8 = bf16[640,2560]{1,0:T(8,128)(2,1)} collective-permute-done((bf16[640,2560]{1,0:T(8,128)(2,1)}, bf16[640,2560]{1,0:T(8,128)(2,1)}, u32[]{:S(2)}, u32[]{:S(2)}) %collective-permute-start.8) | collective-permute-done | bytes 3276832 | tf_op jit(solution)/shard_map/ppermute | solution.py:106
  1093.2 84.6 %collective-permute-done.22 = bf16[320,2560]{1,0:T(8,128)(2,1)S(1)} collective-permute-done((bf16[320,2560]{1,0:T(8,128)(2,1)S(1)}, bf16[320,2560]{1,0:T(8,128)(2,1)S(1)}, u32[]{:S(2)}, u32[]{:S(2)}) %collective-permute-start.22) | collective-permute-done | bytes 1638432 | tf_op jit(solution)/shard_map/ppermute | solution.py:106
  1180.6 32.4 %collective-permute-done.13 = bf16[320,2560]{1,0:T(8,128)(2,1)S(1)} collective-permute-done((bf16[320,2560]{1,0:T(8,128)(2,1)S(1)}, bf16[320,2560]{1,0:T(8,128)(2,1)S(1)}, u32[]{:S(2)}, u32[]{:S(2)}) %collective-permute-start.13) | collective-permute-done | bytes 1638432 | tf_op jit(solution)/shard_map/ppermute | solution.py:106
  1213.6 33.6 %collective-permute-done.9 = bf16[320,2560]{1,0:T(8,128)(2,1)S(1)} collective-permute-done((bf16[320,2560]{1,0:T(8,128)(2,1)S(1)}, bf16[320,2560]{1,0:T(8,128)(2,1)S(1)}, u32[]{:S(2)}, u32[]{:S(2)}) %collective-permute-start.9) | collective-permute-done | bytes 1638432 | tf_op jit(solution)/shard_map/ppermute | solution.py:106
  1248.2 16.6 %collective-permute-done.23 = bf16[160,2560]{1,0:T(8,128)(2,1)S(1)} collective-permute-done((bf16[160,2560]{1,0:T(8,128)(2,1)S(1)}, bf16[160,2560]{1,0:T(8,128)(2,1)S(1)}, u32[]{:S(2)}, u32[]{:S(2)}) %collective-permute-start.23) | collective-permute-done | bytes 819232 | tf_op jit(solution)/shard_map/ppermute | solution.py:106
  1266.1 16.2 %collective-permute-done.14 = bf16[160,2560]{1,0:T(8,128)(2,1)S(1)} collective-permute-done((bf16[160,2560]{1,0:T(8,128)(2,1)S(1)}, bf16[160,2560]{1,0:T(8,128)(2,1)S(1)}, u32[]{:S(2)}, u32[]{:S(2)}) %collective-permute-start.14) | collective-permute-done | bytes 819232 | tf_op jit(solution)/shard_map/ppermute | solution.py:106
  1283.7 16.2 %collective-permute-done.10 = bf16[160,2560]{1,0:T(8,128)(2,1)S(1)} collective-permute-done((bf16[160,2560]{1,0:T(8,128)(2,1)S(1)}, bf16[160,2560]{1,0:T(8,128)(2,1)S(1)}, u32[]{:S(2)}, u32[]{:S(2)}) %collective-permute-start.10) | collective-permute-done | bytes 819232 | tf_op jit(solution)/shard_map/ppermute | solution.py:106
  (455 shorter events, 491.3 us)
Async XLA Ops:
  7.2 86.4 %copy-start = (bf16[2560,256]{1,0:T(8,128)(2,1)S(1)}, bf16[2560,256]{1,0:T(8,128)(2,1)}, u32[]{:S(2)}) copy-start(bf16[2560,256]{1,0:T(8,128)(2,1)} %param.26) | copy-start | bytes 3932164
  7.2 1294.0 %all-reduce.23.cloned.1.call-start = ((), (), s32[]{:S(2)}) async-start(), calls=%async_computation | async-start | bytes 168960 | tf_op jit(solution)/shard_map/psum | solution.py:241
  7.2 6.1 collective-permute-start
  7.8 245.2 %collective-permute-start.3 = (bf16[512,2560]{1,0:T(8,128)(2,1)}, bf16[512,2560]{1,0:T(8,128)(2,1)}, u32[]{:S(2)}, u32[]{:S(2)}) collective-permute-start(bf16[512,2560]{1,0:T(8,128)(2,1)} %bitcast.298), channel_id=1, source_target_pairs={{0,1},{1,0},{2,3},{3,2},{4,5},{5,4},{6,7},{7,6},{8,9},{9,8},{10,11... | collective-permute-start | bytes 7864328 | tf_op jit(solution)/shard_map/ppermute | solution.py:99
  8.6 316.9 %copy-start.60 = (f32[2560]{0:T(1024)}, f32[2560]{0:T(1024)S(1)}, u32[]{:S(2)}) copy-start(f32[2560]{0:T(1024)S(1)} %mul.590) | copy-start | bytes 30724
  13.3 84.4 %copy-start.82 = (f32[1,256]{1,0:T(1,128)}, f32[1,256]{1,0:T(1,128)S(1)}, u32[]{:S(2)}) copy-start(f32[1,256]{1,0:T(1,128)S(1)} %get-tuple-element.417) | copy-start | bytes 3076
  13.3 84.4 %copy-start.84 = (f32[1,256]{1,0:T(1,128)}, f32[1,256]{1,0:T(1,128)S(1)}, u32[]{:S(2)}) copy-start(f32[1,256]{1,0:T(1,128)S(1)} %get-tuple-element.418) | copy-start | bytes 3076
  32.5 106.1 %copy-start.40 = (f32[4,256,40]{1,2,0:T(8,128)}, f32[4,256,40]{1,2,0:T(8,128)S(1)}, u32[]{:S(2)}) copy-start(f32[4,256,40]{1,2,0:T(8,128)S(1)} %get-tuple-element.413) | copy-start | bytes 491524
  252.5 46.9 %collective-permute-start.1 = (f32[1024,1]{0,1:T(1,128)S(1)}, f32[1024,1]{0,1:T(1,128)S(1)}, u32[]{:S(2)}, u32[]{:S(2)}) collective-permute-start(f32[1024,1]{0,1:T(1,128)S(1)} %bitcast.345), channel_id=1, source_target_pairs={{0,1},{1,0},{2,3},{3,2},{4,5},{5,4},{6,7},{7,6},{8,9},{9,8},{10,11... | collective-permute-start | bytes 12296 | tf_op jit(solution)/shard_map/ppermute | solution.py:99
  324.3 1.2 collective-permute-start.4
  731.0 209.2 %collective-permute-start.20 = (bf16[1280,2560]{1,0:T(8,128)(2,1)}, bf16[1280,2560]{1,0:T(8,128)(2,1)}, u32[]{:S(2)}, u32[]{:S(2)}) collective-permute-start(bf16[1280,2560]{1,0:T(8,128)(2,1)} %fusion.136), channel_id=1, source_target_pairs={{0,2},{1,5},{2,0},{3,7},{4,6},{5,1},{6,4},{7,3},{8,10},{9,13},{10,... | collective-permute-start | bytes 19660808 | tf_op jit(solution)/shard_map/ppermute | solution.py:112
  747.9 57.9 %collective-permute-start.5 = (f32[1024,256]{1,0:T(8,128)}, f32[1024,256]{1,0:T(8,128)S(1)}, u32[]{:S(2)}, u32[]{:S(2)}) collective-permute-start(f32[1024,256]{1,0:T(8,128)} %pad_maximum_fusion), channel_id=1, source_target_pairs={{0,1},{1,0},{2,3},{3,2},{4,5},{5,4},{6,7},{7,6},{8,9},{9,8},{10,11... | collective-permute-start | bytes 3145736 | tf_op jit(solution)/shard_map/ppermute | solution.py:99
  757.1 192.6 %collective-permute-start.11 = (bf16[1280,2560]{1,0:T(8,128)(2,1)}, bf16[1280,2560]{1,0:T(8,128)(2,1)}, u32[]{:S(2)}, u32[]{:S(2)}) collective-permute-start(bf16[1280,2560]{1,0:T(8,128)(2,1)} %fusion.134), channel_id=1, source_target_pairs={{0,2},{1,5},{2,0},{3,7},{4,6},{5,1},{6,4},{7,3},{8,10},{9,13},{10,... | collective-permute-start | bytes 19660808 | tf_op jit(solution)/shard_map/ppermute | solution.py:112
  810.2 70.2 %collective-permute-start.15 = (bf16[1280,168]{0,1:T(8,128)(2,1)S(1)}, bf16[1280,168]{0,1:T(8,128)(2,1)S(1)}, u32[]{:S(2)}, u32[]{:S(2)}) collective-permute-start(bf16[1280,168]{0,1:T(8,128)(2,1)S(1)} %fusion.79), channel_id=1, source_target_pairs={{0,2},{1,5},{2,0},{3,7},{4,6},{5,1},{6,4},{7,3},{8,10},{9,13},{10,... | collective-permute-start | bytes 1290248 | tf_op jit(solution)/shard_map/ppermute | solution.py:112
  821.4 96.5 %collective-permute-start.6 = (f32[512,2560]{1,0:T(8,128)}, f32[512,2560]{1,0:T(8,128)}, u32[]{:S(2)}, u32[]{:S(2)}) collective-permute-start(f32[512,2560]{1,0:T(8,128)} %add_add_fusion), channel_id=1, source_target_pairs={{0,1},{1,0},{2,3},{3,2},{4,5},{5,4},{6,7},{7,6},{8,9},{9,8},{10,11... | collective-permute-start | bytes 15728648 | tf_op jit(solution)/shard_map/ppermute | solution.py:99
  821.5 81.8 %collective-permute-start.2 = (bf16[512,2560]{1,0:T(8,128)(2,1)}, bf16[512,2560]{1,0:T(8,128)(2,1)}, u32[]{:S(2)}, u32[]{:S(2)}) collective-permute-start(bf16[512,2560]{1,0:T(8,128)(2,1)} %fusion.65), channel_id=1, source_target_pairs={{0,1},{1,0},{2,3},{3,2},{4,5},{5,4},{6,7},{7,6},{8,9},{9,8},{10,11... | collective-permute-start | bytes 7864328 | tf_op jit(solution)/shard_map/ppermute | solution.py:99
  880.5 6.0 collective-permute-start.16
  886.7 8.2 collective-permute-start.17
  895.0 4.6 collective-permute-start.18
  899.6 1.4 collective-permute-start.19
  901.0 100.4 %collective-permute-start.7 = (bf16[1280,2560]{1,0:T(8,128)(2,1)}, bf16[1280,2560]{1,0:T(8,128)(2,1)}, u32[]{:S(2)}, u32[]{:S(2)}) collective-permute-start(bf16[1280,2560]{1,0:T(8,128)(2,1)} %fusion.132), channel_id=1, source_target_pairs={{0,2},{1,5},{2,0},{3,7},{4,6},{5,1},{6,4},{7,3},{8,10},{9,13},{10,... | collective-permute-start | bytes 19660808 | tf_op jit(solution)/shard_map/ppermute | solution.py:112
  948.1 75.7 %collective-permute-start.21 = (bf16[640,2560]{1,0:T(8,128)(2,1)S(1)}, bf16[640,2560]{1,0:T(8,128)(2,1)}, u32[]{:S(2)}, u32[]{:S(2)}) collective-permute-start(bf16[640,2560]{1,0:T(8,128)(2,1)S(1)} %slice.339), channel_id=1, source_target_pairs={{0,4},{1,3},{2,6},{3,1},{4,0},{5,7},{6,2},{7,5},{8,12},{9,11},{10,... | collective-permute-start | bytes 9830408 | tf_op jit(solution)/shard_map/ppermute | solution.py:106
  967.6 79.7 %collective-permute-start.12 = (bf16[640,2560]{1,0:T(8,128)(2,1)}, bf16[640,2560]{1,0:T(8,128)(2,1)}, u32[]{:S(2)}, u32[]{:S(2)}) collective-permute-start(bf16[640,2560]{1,0:T(8,128)(2,1)} %slice.340), channel_id=1, source_target_pairs={{0,4},{1,3},{2,6},{3,1},{4,0},{5,7},{6,2},{7,5},{8,12},{9,11},{10,... | collective-permute-start | bytes 9830408 | tf_op jit(solution)/shard_map/ppermute | solution.py:106
  1019.2 63.1 %collective-permute-start.8 = (bf16[640,2560]{1,0:T(8,128)(2,1)}, bf16[640,2560]{1,0:T(8,128)(2,1)}, u32[]{:S(2)}, u32[]{:S(2)}) collective-permute-start(bf16[640,2560]{1,0:T(8,128)(2,1)} %slice.341), channel_id=1, source_target_pairs={{0,4},{1,3},{2,6},{3,1},{4,0},{5,7},{6,2},{7,5},{8,12},{9,11},{10,... | collective-permute-start | bytes 9830408 | tf_op jit(solution)/shard_map/ppermute | solution.py:106
  1031.8 146.0 %collective-permute-start.22 = (bf16[320,2560]{1,0:T(8,128)(2,1)S(1)}, bf16[320,2560]{1,0:T(8,128)(2,1)S(1)}, u32[]{:S(2)}, u32[]{:S(2)}) collective-permute-start(bf16[320,2560]{1,0:T(8,128)(2,1)S(1)} %slice.342), channel_id=1, source_target_pairs={{0,16},{1,17},{2,18},{3,19},{4,20},{5,21},{6,22},{7,23},{8,24},{9,... | collective-permute-start | bytes 4915208 | tf_op jit(solution)/shard_map/ppermute | solution.py:106
  1056.8 156.1 %collective-permute-start.13 = (bf16[320,2560]{1,0:T(8,128)(2,1)S(1)}, bf16[320,2560]{1,0:T(8,128)(2,1)S(1)}, u32[]{:S(2)}, u32[]{:S(2)}) collective-permute-start(bf16[320,2560]{1,0:T(8,128)(2,1)S(1)} %slice.343), channel_id=1, source_target_pairs={{0,16},{1,17},{2,18},{3,19},{4,20},{5,21},{6,22},{7,23},{8,24},{9,... | collective-permute-start | bytes 4915208 | tf_op jit(solution)/shard_map/ppermute | solution.py:106
  1088.1 124.9 %slice-start.10 = ((s8[6553600]{0:T(1024)(128)(4,1)}), s8[4194304]{0:T(1024)(128)(4,1)S(1)}, s32[]{:S(2)}) async-start(s8[6553600]{0:T(1024)(128)(4,1)} %bitcast.280), calls=%async_computation.11 | async-start | bytes 8388608
  1090.3 122.6 %slice-start.11 = ((s8[6553600]{0:T(1024)(128)(4,1)}), s8[2359296]{0:T(1024)(128)(4,1)S(1)}, s32[]{:S(2)}) async-start(s8[6553600]{0:T(1024)(128)(4,1)} %bitcast.280), calls=%async_computation.12 | async-start | bytes 4718592
  1090.4 156.9 %collective-permute-start.9 = (bf16[320,2560]{1,0:T(8,128)(2,1)S(1)}, bf16[320,2560]{1,0:T(8,128)(2,1)S(1)}, u32[]{:S(2)}, u32[]{:S(2)}) collective-permute-start(bf16[320,2560]{1,0:T(8,128)(2,1)S(1)} %slice.344), channel_id=1, source_target_pairs={{0,16},{1,17},{2,18},{3,19},{4,20},{5,21},{6,22},{7,23},{8,24},{9,... | collective-permute-start | bytes 4915208 | tf_op jit(solution)/shard_map/ppermute | solution.py:106
  1180.5 84.3 %collective-permute-start.23 = (bf16[160,2560]{1,0:T(8,128)(2,1)S(1)}, bf16[160,2560]{1,0:T(8,128)(2,1)S(1)}, u32[]{:S(2)}, u32[]{:S(2)}) collective-permute-start(bf16[160,2560]{1,0:T(8,128)(2,1)S(1)} %slice.345), channel_id=1, source_target_pairs={{0,8},{1,9},{2,10},{3,11},{4,12},{5,13},{6,14},{7,15},{8,0},{9,1},... | collective-permute-start | bytes 2457608 | tf_op jit(solution)/shard_map/ppermute | solution.py:106
  1213.5 68.8 %collective-permute-start.14 = (bf16[160,2560]{1,0:T(8,128)(2,1)S(1)}, bf16[160,2560]{1,0:T(8,128)(2,1)S(1)}, u32[]{:S(2)}, u32[]{:S(2)}) collective-permute-start(bf16[160,2560]{1,0:T(8,128)(2,1)S(1)} %slice.346), channel_id=1, source_target_pairs={{0,8},{1,9},{2,10},{3,11},{4,12},{5,13},{6,14},{7,15},{8,0},{9,1},... | collective-permute-start | bytes 2457608 | tf_op jit(solution)/shard_map/ppermute | solution.py:106
  1247.7 52.2 %collective-permute-start.10 = (bf16[160,2560]{1,0:T(8,128)(2,1)S(1)}, bf16[160,2560]{1,0:T(8,128)(2,1)S(1)}, u32[]{:S(2)}, u32[]{:S(2)}) collective-permute-start(bf16[160,2560]{1,0:T(8,128)(2,1)S(1)} %slice.347), channel_id=1, source_target_pairs={{0,8},{1,9},{2,10},{3,11},{4,12},{5,13},{6,14},{7,15},{8,0},{9,1},... | collective-permute-start | bytes 2457608 | tf_op jit(solution)/shard_map/ppermute | solution.py:106
  (108 other events, 2739.8 us)
Sparse Core Ops, SparseCore 0:
  940.3 207.9 all-reduce.22
